TPU v7x, 32 devices: a whole 2x2x4 slice. The times are simulated.
32 devices in a mesh: shift: 2 (over y), space: 4 (over z), orb: 2 (over x), grid: 2 (over core).
Axes of the slice: x: 2, y: 2, z: 4, core: 2. Of those that a mesh axis runs over, the one named last changes fastest.
Arguments:
- support: bfloat16 [128, 9, 15, 256], P(('shift', 'space', 'orb'), None, None, 'grid'), parts along dimension 0, may hold values from -0.75 to 0.75
- anchor: int32 [128], P(('shift', 'space', 'orb')), parts along dimension 0, may hold values from 0 to 63, as said below
- kernel: float32 [512, 9, 9], P(('shift', 'space', 'orb')), parts along dimension 0, may hold values from -2.1 to 2.1
- pair_owner: int32 [512], P(('shift', 'space', 'orb')), parts along dimension 0, may hold values from 0 to 63, as said below
- pair_partner: int32 [512], P(('shift', 'space', 'orb')), parts along dimension 0, may hold values from 0 to 63, as said below
- pair_live: int32 [512], P(('shift', 'space', 'orb')), parts along dimension 0, may hold values 0 or 1
- v_ext: float32 [128, 256], P(('shift', 'space'), 'grid'), parts along dimension 0, may hold values from -6 to 6
Outputs:
- density: float32 [128, 256], P(('shift', 'space'), 'grid'), parts along dimension 0
- hamiltonian: float32 [512, 9, 9], P(('shift', 'space', 'orb')), parts along dimension 0
There are 2 independent parts, one for each index of `shift`. A program takes and returns all parts, laid end to end along the dimension named above; each array names one. Nothing has to cross between parts.
Inputs may be any that keep to these rules, and one draw needn't show every extreme that they name: Atom a lies in spatial domain a // 16, and its box starts at a plane of that domain: anchor[a] // 16 = a // 16. The owner of slot p is one of the 8 atoms of block p // 32: pair_owner[p] // 8 = p // 32. `pair_partner`: the partner of a slot lies in its owner's spatial domain or in one of the two adjacent domains, counted periodically, and its box shares at least one plane with the owner's box: |gap| <= 14.
All inputs are finite; a program needn't handle non-finite values. No bound on the sum of `pair_live` on one device may be relied on, other than what follows from the above.
Results may differ from a plain program's by a relative error of at most 0.0028.
Values may be sent and summed in bfloat16 or wider, within the bound.
A program may use at most 64 MiB of HBM per device.

v0:
```python
import jax
import jax.numpy as jnp
from jax import lax
from jax.sharding import PartitionSpec as P


def shifted(value, axis, steps):
    count = lax.axis_size(axis)
    pairs = [(source, (source + steps) % count) for source in range(count)]
    return lax.ppermute(value, axis, pairs)


def shift_planes(rows, plane_gap, box_depth):
    index = jnp.arange(box_depth, dtype=jnp.int32)[None, :] + plane_gap[:, None]
    inside = (index >= 0) & (index < box_depth)
    picked = jnp.take_along_axis(rows, jnp.clip(index, 0, box_depth - 1)[:, None, :, None], axis=2)
    return jnp.where(inside[:, None, :, None], picked, jnp.zeros_like(picked))


def respond(field):
    return field / jnp.sqrt(1.0 + field * field)


def on_device(support, anchor, kernel, pair_owner, pair_partner, pair_live, v_ext):
    per_device, functions, box_depth, points = support.shape
    pair_count = kernel.shape[0]
    slab_rows = v_ext.shape[0]
    orb_count = lax.axis_size("orb")
    space_count = lax.axis_size("space")
    per_domain = per_device * orb_count
    total_planes = slab_rows * space_count
    domain = lax.axis_index("space")
    orb_index = lax.axis_index("orb")
    own_block = domain * orb_count + orb_index
    below_support, below_anchor = shifted((support, anchor), "space", 1)
    above_support, above_anchor = shifted((support, anchor), "space", -1)
    lower_support, domain_support, upper_support, lower_anchor, domain_anchor, upper_anchor = (
        lax.all_gather(below_support, "orb", axis=0, tiled=True),
        lax.all_gather(support, "orb", axis=0, tiled=True),
        lax.all_gather(above_support, "orb", axis=0, tiled=True),
        lax.all_gather(below_anchor, "orb", axis=0, tiled=True),
        lax.all_gather(anchor, "orb", axis=0, tiled=True),
        lax.all_gather(above_anchor, "orb", axis=0, tiled=True),
    )
    window_support = jnp.concatenate([lower_support, domain_support, upper_support], axis=0)
    window_anchor = jnp.concatenate([lower_anchor, domain_anchor, upper_anchor], axis=0)
    partner_domain = pair_partner // per_domain
    relative = (partner_domain - domain + 1 + space_count) % space_count
    window_index = relative * per_domain + pair_partner % per_domain
    owner_local = pair_owner - own_block * per_device
    plane_gap = (
        (anchor[owner_local] - window_anchor[window_index] + total_planes // 2) % total_planes
        - total_planes // 2
    ).astype(jnp.int32)
    alive = pair_live.astype(jnp.float32)
    block_count = pair_count // pair_count
    index_blocks = window_index.reshape(block_count, pair_count)
    gap_blocks = plane_gap.reshape(block_count, pair_count)
    owner_blocks = owner_local.reshape(block_count, pair_count)
    kernel_blocks = (kernel * alive[:, None, None]).reshape(
        block_count, pair_count, functions, functions
    )
    atom_ids = jnp.arange(per_device, dtype=jnp.int32)

    def aux_step(total, items):
        rows_index, gaps, kern, owners = items
        moved = shift_planes(window_support[rows_index], gaps, box_depth)
        terms = jnp.einsum(
            "pst,ptjq->psjq", kern, moved.astype(jnp.float32), precision=lax.Precision.HIGHEST
        )
        table = (owners[None, :] == atom_ids[:, None]).astype(jnp.float32)
        return (
            total + jnp.einsum("ap,psjq->asjq", table, terms, precision=lax.Precision.HIGHEST),
            None,
        )

    start_aux = jnp.zeros((per_device, functions, box_depth, points), jnp.float32)
    aux, _ = lax.scan(aux_step, start_aux, (index_blocks, gap_blocks, kernel_blocks, owner_blocks))
    deposit_terms = jnp.sum(support.astype(jnp.float32) * aux, axis=1)
    offset = anchor - domain * slab_rows
    local_plane = offset[:, None] + jnp.arange(box_depth, dtype=jnp.int32)[None, :]
    placing = (
        jnp.arange(2 * slab_rows, dtype=jnp.int32)[:, None, None] == local_plane[None, :, :]
    ).astype(jnp.float32)
    deposit = jnp.einsum("zaj,ajq->zq", placing, deposit_terms, precision=lax.Precision.HIGHEST)
    summed = lax.psum(deposit, "orb")
    incoming = shifted(summed[slab_rows:], "space", 1)
    density = summed[:slab_rows] + incoming
    potential = v_ext + respond(density)
    next_potential = shifted(potential, "space", -1)
    both_slabs = jnp.concatenate([potential, next_potential], axis=0)
    box_potential = jnp.einsum("zaj,zq->ajq", placing, both_slabs, precision=lax.Precision.HIGHEST)
    weighted = (support.astype(jnp.float32) * box_potential[:, None, :, :]).astype(jnp.bfloat16)

    def ham_block(items):
        rows_index, gaps, owners = items
        moved = shift_planes(window_support[rows_index], gaps, box_depth)
        owner_rows = weighted[owners]
        return jnp.einsum("psjq,ptjq->pst", owner_rows, moved, preferred_element_type=jnp.float32)

    partial_blocks = lax.map(ham_block, (index_blocks, gap_blocks, owner_blocks)).reshape(
        pair_count, functions, functions
    )
    hamiltonian = lax.psum(partial_blocks, "grid") * alive[:, None, None]
    return (density, hamiltonian)


def solution(mesh):
    placed = (
        P(("shift", "space", "orb"), None, None, "grid"),
        P(("shift", "space", "orb")),
        P(("shift", "space", "orb"), None, None),
        P(("shift", "space", "orb")),
        P(("shift", "space", "orb")),
        P(("shift", "space", "orb")),
        P(("shift", "space"), "grid"),
    )
    return jax.shard_map(
        on_device,
        mesh=mesh,
        in_specs=placed,
        out_specs=(P(("shift", "space"), "grid"), P(("shift", "space", "orb"), None, None)),
        check_vma=False,
    )
```

profile of v0, /device:TPU:0, one launch (start us, length us, event | category | flops | bytes accessed | tf_op | source)
XLA Modules:
  0.0 81.6 jit_solution(5677399734707426305)
XLA Ops:
  0.7 3.1 %collective-permute-start = (s32[8]{0:T(128)}, s32[8]{0:T(128)S(1)}, u32[]{:S(2)}, u32[]{:S(2)}) collective-permute-start(s32[8]{0:T(128)} %param.10), channel_id=1, source_target_pairs={{0,4},{4,8},{8,12},{12,0},{1,5},{5,9},{9,13},{13,1},{2,6},{6,10},{... | collective-permute-start | bytes 104 | tf_op jit(solution)/shard_map/ppermute | solution.py:10
  3.8 2.1 %collective-permute-start.1 = (s32[8]{0:T(128)}, s32[8]{0:T(128)S(1)}, u32[]{:S(2)}, u32[]{:S(2)}) collective-permute-start(s32[8]{0:T(128)} %param.10), channel_id=1, source_target_pairs={{0,12},{4,0},{8,4},{12,8},{1,13},{5,1},{9,5},{13,9},{2,14},{6,2},{... | collective-permute-start | bytes 104 | tf_op jit(solution)/shard_map/ppermute | solution.py:10
  5.9 3.8 %collective-permute-start.3 = (bf16[8,9,15,128]{3,0,2,1:T(8,128)(2,1)}, bf16[8,9,15,128]{3,0,2,1:T(8,128)(2,1)S(1)}, u32[]{:S(2)}, u32[]{:S(2)}) collective-permute-start(bf16[8,9,15,128]{3,0,2,1:T(8,128)(2,1)} %param.9), channel_id=1, source_target_pairs={{0,12},{4,0},{8,4},{12,8},{1,13},{5,1},{9,5},{13,9},{2,14},{6,2},{... | collective-permute-start | bytes 829448 | tf_op jit(solution)/shard_map/ppermute | solution.py:10
  9.7 8.4 %all_gather.22 = bf16[16,9,15,128]{3,0,2,1:T(8,128)(2,1)S(1)} all-gather(bf16[8,9,15,128]{3,0,2,1:T(8,128)(2,1)} %param.9), channel_id=1, replica_groups=mesh['shift'=2,'space'=4,'orb'=2,'grid'=2] {'orb'}, dimensions={0}, use_global_device_ids=true | all-gather | bytes 829440 | tf_op jit(solution)/shard_map/all_gather | solution.py:39
  18.1 0.7 compare_select_fusion.1
  18.8 0.7 compare_select_fusion.2
  19.5 1.4 %gather_fusion = s32[32]{0:T(128)S(1)} fusion(s32[8]{0:T(128)} %param.10, s32[1024]{0:T(1024)S(1)} %pad_clamp_fusion.1), kind=kCustom, calls=%fused_computation.1 | custom fusion | bytes 384 | tf_op jit(solution)/shard_map/gather | solution.py:52
  21.3 0.6 dynamic-slice.4
  22.6 0.2 dynamic-update-slice.1
  22.8 0.2 dynamic-update-slice
  23.1 0.2 dynamic-update-slice.2
  23.3 4.3 %all-reduce.3 = (s32[16]{0:T(128)S(1)}, s32[16]{0:T(128)S(1)}, s32[16]{0:T(128)S(1)}) all-reduce(s32[16]{0:T(128)S(1)} %dynamic-update-slice.2, s32[16]{0:T(128)S(1)} %dynamic-update-slice.1, s32[16]{0:T(128)S(1)} %dynamic-update-slice), channel_id=1, replica_groups=mesh['shift'=2,'space'=4,'orb'=2,'grid'=2] {'orb'}, use_global_device_ids=true, to_apply=%add.2 | all-reduce | flops 48 | bytes 384
  27.6 0.7 gather_fusion.1
  28.7 8.0 %all_gather.21 = bf16[16,9,15,128]{3,0,2,1:T(8,128)(2,1)S(1)} all-gather(bf16[8,9,15,128]{3,0,2,1:T(8,128)(2,1)S(1)} %collective-permute-done.2), channel_id=1, replica_groups=mesh['shift'=2,'space'=4,'orb'=2,'grid'=2] {'orb'}, dimensions={0}, use_global_device_ids=true | all-gather | bytes 829440 | tf_op jit(solution)/shard_map/all_gather | solution.py:38
  36.8 7.2 %all_gather.23 = bf16[16,9,15,128]{3,0,2,1:T(8,128)(2,1)S(1)} all-gather(bf16[8,9,15,128]{3,0,2,1:T(8,128)(2,1)S(1)} %collective-permute-done.3), channel_id=1, replica_groups=mesh['shift'=2,'space'=4,'orb'=2,'grid'=2] {'orb'}, dimensions={0}, use_global_device_ids=true | all-gather | bytes 829440 | tf_op jit(solution)/shard_map/all_gather | solution.py:40
  44.2 0.3 pad_maximum_fusion
  44.5 0.8 gather_fusion.2
  45.3 1.8 %copy.40 = bf16[32,9,15,128]{3,1,2,0:T(8,128)(2,1)} copy(bf16[32,9,15,128]{3,2,1,0:T(8,128)(2,1)S(1)} %gather_fusion.2) | data formatting | bytes 2211840 | tf_op jit(solution)/shard_map/while/body/eval_jaxpr/gather | solution.py:67
  47.1 5.2 %gather_fusion.4 = bf16[480,9,128]{2,1,0:T(8,128)(2,1)S(1)} fusion(bf16[32,9,15,128]{3,1,2,0:T(8,128)(2,1)} %copy.40, s32[480]{0:T(512)S(1)} %reshape.174), kind=kCustom, calls=%fused_computation.clone | custom fusion | bytes 2215680 | tf_op jit(solution)/shard_map/while/body/eval_jaxpr/jit(take_along_axis)/gather | solution.py:16
  52.3 0.3 bitcast_select_fusion
  52.7 2.1 %fusion.4 = f32[32,9,15,128]{3,1,2,0:T(8,128)S(1)} fusion(bf16[32,9,15,128]{3,2,0,1:T(8,128)(2,1)S(1)} %bitcast_select_fusion, f32[32,9,9]{2,1,0:T(8,128)S(1)} %copy.36, f32[32]{0:T(128)S(1)} %convert_element_type.16), kind=kOutput, calls=%fused_computation.9 | convolution fusion | flops 59722272 | bytes 3328256 | tf_op jit(solution)/shard_map/while/body/eval_jaxpr/pst,ptjq->psjq/dot_general | solution.py:68
  54.8 1.5 %fusion.10 = f32[8,15,128]{2,0,1:T(8,128)S(1)} fusion(f32[32,9,15,128]{3,1,2,0:T(8,128)S(1)} %fusion.4, bf16[8,9,15,128]{3,0,2,1:T(8,128)(2,1)S(1)} %copy-done.1, s32[32]{0:T(128)S(1)} %get-tuple-element.62), kind=kOutput, calls=%fused_computation.14 | convolution fusion | flops 53483776 | bytes 2549888 | tf_op jit(solution)/shard_map/while/body/eval_jaxpr/ap,psjq->asjq/dot_general | solution.py:73
  56.3 0.3 convolution_bitcast_fusion
  56.6 8.3 %psum.14 = f32[32,128]{1,0:T(8,128)S(1)} all-reduce(f32[32,128]{1,0:T(8,128)S(1)} %convolution_bitcast_fusion), channel_id=1, replica_groups=mesh['shift'=2,'space'=4,'orb'=2,'grid'=2] {'orb'}, use_global_device_ids=true, to_apply=%region_1.3 | all-reduce | flops 4096 | bytes 32768 | tf_op jit(solution)/shard_map/psum | solution.py:86
  64.9 5.4 %collective-permute-done.4 = f32[16,128]{1,0:T(8,128)S(1)} collective-permute-done((f32[16,128]{1,0:T(8,128)S(1)}, f32[16,128]{1,0:T(8,128)S(1)}, u32[]{:S(2)}, u32[]{:S(2)}) %collective-permute-start.4) | collective-permute-done | bytes 8224 | tf_op jit(solution)/shard_map/ppermute | solution.py:10
  70.4 0.6 multiply_add_fusion
  71.1 3.6 %collective-permute-done.5 = f32[16,128]{1,0:T(8,128)S(1)} collective-permute-done((f32[16,128]{1,0:T(8,128)S(1)}, f32[16,128]{1,0:T(8,128)S(1)}, u32[]{:S(2)}, u32[]{:S(2)}) %collective-permute-start.5) | collective-permute-done | bytes 8224 | tf_op jit(solution)/shard_map/ppermute | solution.py:10
  74.6 0.2 fusion.23
  74.9 0.8 gather_fusion.3
  75.7 1.0 %fusion.13 = f32[32,9,9]{2,1,0:T(8,128)S(1)} fusion(bf16[32,9,15,128]{3,2,0,1:T(8,128)(2,1)S(1)} %bitcast_select_fusion, bf16[32,9,15,128]{3,2,1,0:T(8,128)(2,1)S(1)} %gather_fusion.3), kind=kOutput, calls=%fused_computation.17 | convolution fusion | flops 9953280 | bytes 2222208 | tf_op jit(solution)/shard_map/while/body/eval_jaxpr/psjq,ptjq->pst/dot_general | solution.py:99
  76.7 4.0 %psum.15 = f32[32,9,9]{2,1,0:T(8,128)S(1)} all-reduce(f32[32,9,9]{2,1,0:T(8,128)S(1)} %fusion.13), channel_id=1, replica_groups=mesh['shift'=2,'space'=4,'orb'=2,'grid'=2] {'grid'}, use_global_device_ids=true, to_apply=%region_2.4 | all-reduce | flops 2592 | bytes 20736 | tf_op jit(solution)/shard_map/psum | solution.py:104
  80.8 0.8 copy.49
  (42 shorter events, 1.6 us)
Async XLA Ops:
  0.6 20.7 %copy-start.5 = (u32[32]{0:T(128)S(1)}, u32[32]{0:T(128)}, u32[]{:S(2)}) copy-start(u32[32]{0:T(128)} %constant.154) | copy-start | bytes 388
  0.6 20.6 %copy-start = (s32[8]{0:T(128)S(1)}, s32[8]{0:T(128)}, u32[]{:S(2)}) copy-start(s32[8]{0:T(128)} %param.10) | copy-start | bytes 100
  0.7 20.3 %copy-start.4 = (s32[32]{0:T(128)S(1)}, s32[32]{0:T(128)}, u32[]{:S(2)}) copy-start(s32[32]{0:T(128)} %param.14) | copy-start | bytes 388
  0.7 20.4 %copy-start.2 = (f32[32,9,9]{0,2,1:T(8,128)S(1)}, f32[32,9,9]{0,2,1:T(8,128)}, u32[]{:S(2)}) copy-start(f32[32,9,9]{0,2,1:T(8,128)} %param.11) | copy-start | bytes 31108
  0.7 22.1 %collective-permute-start = (s32[8]{0:T(128)}, s32[8]{0:T(128)S(1)}, u32[]{:S(2)}, u32[]{:S(2)}) collective-permute-start(s32[8]{0:T(128)} %param.10), channel_id=1, source_target_pairs={{0,4},{4,8},{8,12},{12,0},{1,5},{5,9},{9,13},{13,1},{2,6},{6,10},{... | collective-permute-start | bytes 104 | tf_op jit(solution)/shard_map/ppermute | solution.py:10
  3.8 19.3 %collective-permute-start.1 = (s32[8]{0:T(128)}, s32[8]{0:T(128)S(1)}, u32[]{:S(2)}, u32[]{:S(2)}) collective-permute-start(s32[8]{0:T(128)} %param.10), channel_id=1, source_target_pairs={{0,12},{4,0},{8,4},{12,8},{1,13},{5,1},{9,5},{13,9},{2,14},{6,2},{... | collective-permute-start | bytes 104 | tf_op jit(solution)/shard_map/ppermute | solution.py:10
  5.9 22.8 %collective-permute-start.2 = (bf16[8,9,15,128]{3,0,2,1:T(8,128)(2,1)}, bf16[8,9,15,128]{3,0,2,1:T(8,128)(2,1)S(1)}, u32[]{:S(2)}, u32[]{:S(2)}) collective-permute-start(bf16[8,9,15,128]{3,0,2,1:T(8,128)(2,1)} %param.9), channel_id=1, source_target_pairs={{0,4},{4,8},{8,12},{12,0},{1,5},{5,9},{9,13},{13,1},{2,6},{6,10},{... | collective-permute-start | bytes 829448 | tf_op jit(solution)/shard_map/ppermute | solution.py:10
  5.9 30.9 %collective-permute-start.3 = (bf16[8,9,15,128]{3,0,2,1:T(8,128)(2,1)}, bf16[8,9,15,128]{3,0,2,1:T(8,128)(2,1)S(1)}, u32[]{:S(2)}, u32[]{:S(2)}) collective-permute-start(bf16[8,9,15,128]{3,0,2,1:T(8,128)(2,1)} %param.9), channel_id=1, source_target_pairs={{0,12},{4,0},{8,4},{12,8},{1,13},{5,1},{9,5},{13,9},{2,14},{6,2},{... | collective-permute-start | bytes 829448 | tf_op jit(solution)/shard_map/ppermute | solution.py:10
  52.7 2.1 %copy-start.1 = (bf16[8,9,15,128]{3,0,2,1:T(8,128)(2,1)S(1)}, bf16[8,9,15,128]{3,0,2,1:T(8,128)(2,1)}, u32[]{:S(2)}) copy-start(bf16[8,9,15,128]{3,0,2,1:T(8,128)(2,1)} %param.9) | copy-start | bytes 829444
  54.7 15.6 %copy-start.3 = (f32[16,128]{1,0:T(8,128)S(1)}, f32[16,128]{1,0:T(8,128)}, u32[]{:S(2)}) copy-start(f32[16,128]{1,0:T(8,128)} %param.15) | copy-start | bytes 24580
  64.9 5.5 %collective-permute-start.4 = (f32[16,128]{1,0:T(8,128)S(1)}, f32[16,128]{1,0:T(8,128)S(1)}, u32[]{:S(2)}, u32[]{:S(2)}) collective-permute-start(f32[16,128]{1,0:T(8,128)S(1)} %slice.19), channel_id=1, source_target_pairs={{0,4},{4,8},{8,12},{12,0},{1,5},{5,9},{9,13},{13,1},{2,6},{6,10},{... | collective-permute-start | bytes 24584 | tf_op jit(solution)/shard_map/ppermute | solution.py:10
  71.0 3.7 %collective-permute-start.5 = (f32[16,128]{1,0:T(8,128)S(1)}, f32[16,128]{1,0:T(8,128)S(1)}, u32[]{:S(2)}, u32[]{:S(2)}) collective-permute-start(f32[16,128]{1,0:T(8,128)S(1)} %get-tuple-element.52), channel_id=1, source_target_pairs={{0,12},{4,0},{8,4},{12,8},{1,13},{5,1},{9,5},{13,9},{2,14},{6,2},{... | collective-permute-start | bytes 24584 | tf_op jit(solution)/shard_map/ppermute | solution.py:10
where the time goes:
time: 81.8 us; the launch traced here: 81.6 us
  blocking collectives  40.2 us (49%)
  local copies, waits for them, and re-layouts  13.5 us (17%)
  starting transfers between devices  9.06 us (11%)
  waiting for transfers between devices  9 us (11%)
  matrix products  5.04 us (6%)
  other arithmetic  3.28 us (4%)
  between operations  1.56 us (2%)
    ppermute x6, starting transfers between devices, shifted(): return lax.ppermute(value, axis, pairs)  9.06 us
    ppermute x6, waiting for transfers between devices, shifted(): return lax.ppermute(value, axis, pairs)  9 us
    all_gather x1, blocking collectives, on_device(): lax.all_gather(support, 'orb', axis=0, tiled=True)  8.41 us
    psum x1, blocking collectives, on_device(): summed = lax.psum(deposit, 'orb')  8.3 us
    all_gather x1, blocking collectives, on_device(): lax.all_gather(below_support, 'orb', axis=0, tiled=True)  7.96 us
    all_gather x1, blocking collectives, on_device(): lax.all_gather(above_support, 'orb', axis=0, tiled=True)  7.22 us
    gather x2, local copies, waits for them, and re-layouts, shift_planes(): jnp.take_along_axis(rows, jnp.clip(index, 0, box_depth - 1)[:, None, :, N...  5.33 us
    unnamed x1, blocking collectives  4.25 us
  transfers between devices with their start and end apart: 6, of which 2 were waited for; matrix products, arithmetic and copies ran while one was open for 7% of the time, Pallas kernels for 0%

commit v1 on v0

v1 whole, which is shorter than its diff:
```python
import functools

import jax
import jax.numpy as jnp
from jax import lax
from jax.experimental import pallas as pl
from jax.experimental.pallas import tpu as pltpu
from jax.sharding import PartitionSpec as P

LANES = 128
MESH = pl.DeviceIdType.MESH
F32 = jnp.float32
BF16 = jnp.bfloat16


def dot(a, b):
    return lax.dot_general(a, b, (((1,), (0,)), ((), ())), preferred_element_type=F32)


def dot_t(a, b):
    return lax.dot_general(a, b, (((1,), (1,)), ((), ())), preferred_element_type=F32)


def split(value):
    high = value.astype(BF16)
    return high, (value - high.astype(F32)).astype(BF16)


def respond(field):
    return field / jnp.sqrt(1.0 + field * field)


class Plan:
    def __init__(self, support, kernel, v_ext, orbs, spaces):
        self.atoms, self.funcs, self.depth, self.points = support.shape
        self.pairs = kernel.shape[0]
        self.slab = v_ext.shape[0]
        self.orbs, self.spaces = orbs, spaces
        self.blocks = 2 * orbs
        self.rows = self.slab // orbs
        self.width = self.rows * self.points
        self.block = (self.funcs + self.funcs % 2) * self.atoms
        self.total = self.blocks * self.block
        over = self.depth - 1
        self.even = over % orbs == 0 and (self.slab - over) % orbs == 0
        self.zrows = over // orbs if self.even else self.rows
        self.square = self.funcs * self.funcs
        self.over = over
        cut = (self.zrows + 1) // 2
        self.chunks = [(0, cut), (cut, self.zrows)]
        if self.zrows < self.rows:
            self.chunks.append((self.zrows, self.rows))

    def plane(self, orb, i):
        if not self.even:
            return orb * self.rows + i
        if i < self.zrows:
            return orb * self.zrows + i
        return self.over + orb * (self.rows - self.zrows) + i - self.zrows


def body(
    pn,
    meta_ref,
    support_ref,
    v_ref,
    density_ref,
    ham_ref,
    pad,
    packed,
    boxes,
    metas,
    masked,
    kmat,
    aux,
    gmat,
    weighted,
    dens,
    hpart,
    hrecv,
    xs_sem,
    xr_sem,
    zs_sem,
    zr_sem,
    ms_sem,
    mr_sem,
    ds_sem,
    dr_sem,
    hs_sem,
    hr_sem,
):
    n, space_count = pn.orbs, pn.spaces
    A, F, Q = pn.atoms, pn.funcs, pn.points
    orb, dom, grid = lax.axis_index("orb"), lax.axis_index("space"), lax.axis_index("grid")
    above, below = lax.rem(dom + 1, space_count), lax.rem(dom + space_count - 1, space_count)

    def peer(k):
        return lax.rem(orb + k, n)

    barrier = pltpu.get_barrier_semaphore()
    met = 0
    for place in (dom, above, below):
        for k in range(n):
            for g in range(2):
                if place is dom and k == 0 and g == 0:
                    continue
                pl.semaphore_signal(
                    barrier,
                    inc=1,
                    device_id={"space": place, "orb": peer(k), "grid": lax.rem(grid + g, 2)},
                    device_id_type=MESH,
                )
                met += 1

    pad[...] = jnp.zeros_like(pad)
    pad[:, :, 0 : pn.depth, :] = support_ref[...]
    step = pad.shape[2]
    lane = lax.broadcasted_iota(jnp.int32, (A, A * step), 1)
    sub = lax.broadcasted_iota(jnp.int32, (A, A * step), 0)
    j = lane - sub * step
    mine = (j >= 0) & (j < pn.depth)
    offset = jnp.broadcast_to(meta_ref[0:A, pn.square + 3 : pn.square + 4], (A, A * step))
    spot = offset.astype(jnp.int32) + j
    place_rows = []
    for o in range(n):
        for i in range(pn.rows):
            r = pn.plane(o, i)
            hit = mine & ((spot == r) | (spot == r + pn.slab))
            place_rows.append(jnp.where(hit, 1.0, 0.0))
    placing = jnp.concatenate(place_rows, axis=0).astype(BF16)
    aligned = []
    for s in range(F):
        aligned.append(dot(placing, pad[:, s].reshape(A * step, Q)))
    nothing = jnp.zeros((A, Q), F32)
    for o in range(n):
        for i in range(pn.rows):
            base = (o * pn.rows + i) * A
            for s in range(0, F, 2):
                first = aligned[s][base : base + A]
                second = aligned[s + 1][base : base + A] if s + 1 < F else nothing
                packed[o, s * A : (s + 2) * A, i * Q : (i + 1) * Q] = jnp.concatenate(
                    [first, second], axis=0
                ).astype(BF16)

    pl.semaphore_wait(barrier, met)

    sends = []

    def send(src, dst, ssem, rsem, where):
        copy = pltpu.make_async_remote_copy(
            src_ref=src, dst_ref=dst, send_sem=ssem, recv_sem=rsem,
            device_id=where, device_id_type=MESH,
        )
        copy.start()
        sends.append(copy)

    def arrive(dst, ssem, rsem):
        pltpu.make_async_remote_copy(
            src_ref=dst, dst_ref=dst, send_sem=ssem, recv_sem=rsem,
            device_id={"space": above}, device_id_type=MESH,
        ).wait_recv()

    for k in range(1, n):
        send(meta_ref, metas.at[n + orb], ms_sem.at[k], mr_sem.at[n + orb], {"orb": peer(k)})
    for k in range(n):
        send(
            meta_ref, metas.at[orb], ms_sem.at[n + k], mr_sem.at[orb],
            {"space": above, "orb": peer(k)},
        )
    for c, (lo, hi) in enumerate(pn.chunks):
        cols = pl.ds(lo * Q, (hi - lo) * Q)
        for k in range(1, n):
            send(
                packed.at[peer(k), :, cols], boxes.at[n + orb, :, cols],
                xs_sem.at[k, c], xr_sem.at[orb, c], {"orb": peer(k)},
            )
        if c < 2:
            send(
                packed.at[orb, :, cols], boxes.at[orb, :, cols],
                zs_sem.at[0, c], zr_sem.at[orb, c], {"space": above},
            )
    boxes[n + orb] = packed[orb]
    metas[n + orb] = meta_ref[...]
    for c, (lo, hi) in enumerate(pn.chunks):
        cols = pl.ds(lo * Q, (hi - lo) * Q)
        for k in range(1, n):
            other = peer(k)
            arrive(boxes.at[n + other, :, cols], xs_sem.at[k, c], xr_sem.at[other, c])
            if c < 2:
                send(
                    boxes.at[n + other, :, cols], boxes.at[other, :, cols],
                    zs_sem.at[k, c], zr_sem.at[other, c], {"space": above},
                )
    for k in range(1, n):
        other = peer(k)
        arrive(metas.at[n + other], ms_sem.at[k], mr_sem.at[n + other])
    for o in range(n):
        arrive(metas.at[o], ms_sem.at[n], mr_sem.at[o])

    everyone = pn.blocks * pn.pairs
    table = metas[...].reshape(everyone, LANES)
    holder = lax.broadcasted_iota(jnp.int32, (everyone, 1), 0) // pn.pairs
    partner = table[:, pn.square : pn.square + 1].astype(jnp.int32)
    partner = partner - jnp.where(holder < n, n * A, 0)
    owner = table[:, pn.square + 1 : pn.square + 2].astype(jnp.int32) + holder * A

    def columns(shape, axis):
        col = lax.broadcasted_iota(jnp.int32, shape, axis)
        blk = jnp.zeros(shape, jnp.int32)
        for b in range(1, pn.blocks):
            blk = blk + jnp.where(col >= b * pn.block, 1, 0)
        rest = col - blk * pn.block
        func = rest // A
        return blk * A + (rest - func * A), func

    code, func = columns((everyone, pn.total), 1)
    picks = jnp.where((code == partner) & (func < F), 1.0, 0.0)
    picks16 = picks.astype(BF16)
    owner_lane = lax.broadcasted_iota(jnp.int32, (everyone, LANES), 1)
    owns = jnp.where(owner_lane == owner, 1.0, 0.0)
    owns_t = owns.T[0 : pn.blocks * A].astype(BF16)
    owns16 = owns[:, 0 : pn.blocks * A].astype(BF16)
    table_hi, table_lo = split(table)
    spread_row = lax.broadcasted_iota(jnp.int32, (LANES, pn.total), 0)
    _, spread_func = columns((LANES, pn.total), 1)
    spread_func = jnp.where(spread_func < F, spread_func, -pn.square)
    kmat[...] = jnp.zeros_like(kmat)
    for s in range(F):
        spread = jnp.where(spread_row == s * F + spread_func, 1.0, 0.0).astype(BF16)
        q_hi = dot(table_hi, spread).astype(BF16) * picks16
        q_lo = dot(table_lo, spread).astype(BF16) * picks16
        rows = dot(owns_t, q_hi) + dot(owns_t, q_lo)
        for b in range(pn.blocks):
            kmat[b * pn.block + s * A : b * pn.block + (s + 1) * A, :] = rows[b * A : (b + 1) * A]
    k_hi, k_lo = split(kmat[...])

    for k in range(n):
        other = peer(k)
        for c, (lo, hi) in enumerate(pn.chunks[:2]):
            cols = pl.ds(lo * Q, (hi - lo) * Q)
            arrive(boxes.at[other, :, cols], zs_sem.at[k, c], zr_sem.at[other, c])

    for b in range(pn.blocks):
        start = jnp.broadcast_to(metas[b, 0:A, pn.square + 3 : pn.square + 4], (A, Q))
        start = jnp.concatenate([start] * 2, axis=0).astype(jnp.int32)
        for i in range(pn.rows):
            cols = slice(i * Q, (i + 1) * Q)
            if b < n and i >= pn.zrows:
                masked[b * pn.block : (b + 1) * pn.block, cols] = jnp.zeros((pn.block, Q), BF16)
                continue
            r = pn.plane(orb, i)
            keep = (start <= r) if b >= n else (start > r)
            for t in range(pn.block // (2 * A)):
                part = boxes[b, t * 2 * A : (t + 1) * 2 * A, cols].astype(F32)
                masked[b * pn.block + t * 2 * A : b * pn.block + (t + 1) * 2 * A, cols] = jnp.where(
                    keep, part, 0.0
                ).astype(BF16)

    aux[...] = dot(k_hi, masked[...]) + dot(k_lo, masked[...])
    for i in range(pn.rows):
        cols = slice(i * Q, (i + 1) * Q)
        x = masked[:, cols].astype(F32)
        line = jnp.sum(x * aux[:, cols], axis=0, keepdims=True)
        dens[orb, pl.ds(i, 1), :] = line
        potential = v_ref[pl.ds(pn.plane(orb, i), 1), :] + respond(line)
        weighted[:, cols] = (x * potential).astype(BF16)
    for k in range(1, n):
        send(dens.at[orb], dens.at[orb], ds_sem.at[k], dr_sem.at[orb], {"orb": peer(k)})
    gmat[...] = dot_t(weighted[...], masked[...])

    gather_col = lax.broadcasted_iota(jnp.int32, (pn.total, LANES), 1)
    _, gather_func = columns((pn.total, LANES), 0)
    gather_func = jnp.where(gather_func < F, gather_func, -pn.square)
    found = jnp.zeros((everyone, LANES), F32)
    for s in range(F):
        rows = jnp.concatenate(
            [gmat[b * pn.block + s * A : b * pn.block + (s + 1) * A, :] for b in range(pn.blocks)],
            axis=0,
        )
        r_hi, r_lo = split(rows)
        t_hi, t_lo = split((dot(owns16, r_hi) + dot(owns16, r_lo)) * picks)
        gather = jnp.where(gather_col == s * F + gather_func, 1.0, 0.0).astype(BF16)
        found = found + dot(t_hi, gather) + dot(t_lo, gather)
    hpart[...] = found.reshape(pn.blocks, pn.pairs, LANES)

    count = 0
    for up in (1, 0):
        for k in range(n):
            for g in range(2):
                if up == 0 and k == 0 and g == 0:
                    continue
                blk = peer(k) if up else n + peer(k)
                slot = (up * n + orb) * 2 + grid
                send(
                    hpart.at[blk], hrecv.at[slot], hs_sem.at[count], hr_sem.at[slot],
                    {
                        "space": below if up else dom,
                        "orb": peer(k),
                        "grid": lax.rem(grid + g, 2),
                    },
                )
                count += 1
    hrecv[orb * 2 + grid] = hpart[n + orb]
    for k in range(1, n):
        other = peer(k)
        arrive(dens.at[other], ds_sem.at[k], dr_sem.at[other])
    for o in range(n):
        for i in range(pn.rows):
            r = pn.plane(o, i)
            density_ref[r : r + 1, :] = dens[o, i : i + 1, :]
    for up in (0, 1):
        for k in range(n):
            for g in range(2):
                if up == 0 and k == 0 and g == 0:
                    continue
                slot = (up * n + peer(k)) * 2 + lax.rem(grid + g, 2)
                arrive(hrecv.at[slot], hs_sem.at[0], hr_sem.at[slot])
    total = hrecv[0]
    for slot in range(1, 2 * pn.blocks):
        total = total + hrecv[slot]
    ham_ref[...] = total * meta_ref[:, pn.square + 2 : pn.square + 3]
    for copy in sends:
        copy.wait_send()


def on_device(support, anchor, kernel, pair_owner, pair_partner, pair_live, v_ext):
    orb_count, space_count = lax.axis_size("orb"), lax.axis_size("space")
    pn = Plan(support, kernel, v_ext, orb_count, space_count)
    domain, orb_index = lax.axis_index("space"), lax.axis_index("orb")
    per_domain = pn.atoms * orb_count
    own_block = domain * orb_count + orb_index
    partner_domain = pair_partner // per_domain
    relative = (partner_domain - domain + 1 + space_count) % space_count
    code = relative * per_domain + pair_partner % per_domain
    owner = pair_owner - own_block * pn.atoms
    alive = pair_live.astype(F32)
    offset = jnp.pad((anchor - domain * pn.slab).astype(F32), (0, pn.pairs - pn.atoms))
    meta = jnp.concatenate(
        [
            (kernel * alive[:, None, None]).reshape(pn.pairs, pn.square),
            jnp.stack([code.astype(F32), owner.astype(F32), alive, offset], axis=1),
            jnp.zeros((pn.pairs, LANES - pn.square - 4), F32),
        ],
        axis=1,
    )
    n, C = pn.orbs, len(pn.chunks)
    vmem = pl.BlockSpec(memory_space=pltpu.VMEM)
    dma = pltpu.SemaphoreType.DMA
    step = -(-pn.depth // 16) * 16
    density, packed = pl.pallas_call(
        functools.partial(body, pn),
        out_shape=(
            jax.ShapeDtypeStruct(v_ext.shape, F32),
            jax.ShapeDtypeStruct((pn.pairs, LANES), F32),
        ),
        in_specs=[vmem] * 3,
        out_specs=(vmem, vmem),
        scratch_shapes=[
            pltpu.VMEM((pn.atoms, pn.funcs, step, pn.points), BF16),
            pltpu.VMEM((n, pn.block, pn.width), BF16),
            pltpu.VMEM((pn.blocks, pn.block, pn.width), BF16),
            pltpu.VMEM((pn.blocks, pn.pairs, LANES), F32),
            pltpu.VMEM((pn.total, pn.width), BF16),
            pltpu.VMEM((pn.total, pn.total), F32),
            pltpu.VMEM((pn.total, pn.width), F32),
            pltpu.VMEM((pn.total, pn.total), F32),
            pltpu.VMEM((pn.total, pn.width), BF16),
            pltpu.VMEM((n, pn.rows, pn.points), F32),
            pltpu.VMEM((pn.blocks, pn.pairs, LANES), F32),
            pltpu.VMEM((2 * pn.blocks, pn.pairs, LANES), F32),
            dma((n, C)),
            dma((n, C)),
            dma((n, 2)),
            dma((n, 2)),
            dma((2 * n,)),
            dma((2 * n,)),
            dma((n,)),
            dma((n,)),
            dma((2 * pn.blocks,)),
            dma((2 * pn.blocks,)),
        ],
        compiler_params=pltpu.CompilerParams(collective_id=0, has_side_effects=True),
        name="grain",
    )(meta, support, v_ext)
    hamiltonian = packed[:, : pn.square].reshape(pn.pairs, pn.funcs, pn.funcs)
    return (density, hamiltonian)


def solution(mesh):
    placed = (
        P(("shift", "space", "orb"), None, None, "grid"),
        P(("shift", "space", "orb")),
        P(("shift", "space", "orb"), None, None),
        P(("shift", "space", "orb")),
        P(("shift", "space", "orb")),
        P(("shift", "space", "orb")),
        P(("shift", "space"), "grid"),
    )
    return jax.shard_map(
        on_device,
        mesh=mesh,
        in_specs=placed,
        out_specs=(P(("shift", "space"), "grid"), P(("shift", "space", "orb"), None, None)),
        check_vma=False,
    )
```

time: 81.8 us -> 32.5 us (0.40)
  blocking collectives: 40.2 us -> 0 us
  Pallas kernels: 0 us -> 24.7 us
  local copies, waits for them, and re-layouts: 13.5 us -> 4.02 us
  starting transfers between devices: 9.06 us -> 0 us
  waiting for transfers between devices: 9 us -> 0 us
  matrix products: 5.04 us -> 0 us
  between operations: 1.56 us -> 0.68 us
    pallas_call x0 -> x1, Pallas kernels: none -> 24.7 us  [on_device(): pl.pallas_call(functools.partial(body, pn), out_shape=(jax.ShapeDtypeStru...]
    all_gather x3 -> x0, blocking collectives: 23.6 us -> none  [the longest x1 8.41 us: on_device(): lax.all_gather(support, 'orb', axis=0, tiled=True)]
    psum x2 -> x0, blocking collectives: 12.3 us -> none  [the longest x1 8.3 us: on_device(): summed = lax.psum(deposit, 'orb')]
    gather x7 -> x0, local copies, waits for them, and re-layouts: 10.7 us -> none  [the longest x2 5.33 us: shift_planes(): jnp.take_along_axis(rows, jnp.clip(index, 0, box_depth - 1)[:, None, :, N...]
    ppermute x6 -> x0, starting transfers between devices: 9.06 us -> none  [shifted(): return lax.ppermute(value, axis, pairs)]
    ppermute x6 -> x0, waiting for transfers between devices: 9 us -> none  [shifted(): return lax.ppermute(value, axis, pairs)]
    dot_general x5 -> x0, matrix products: 5.04 us -> none  [the longest x1 2.06 us: aux_step(): jnp.einsum('pst,ptjq->psjq', kern, moved.astype(jnp.float32), precision=l...]
    unnamed x1 -> x0, blocking collectives: 4.25 us -> none
  transfers between devices with their start and end apart: 6 -> 0, of which waited for: 2 -> 0; matrix products, arithmetic and copies ran while one was open for 7% -> 0% of each run, Pallas kernels for 0% -> 0%
where the time goes in v1:
time: 32.5 us; the launch traced here: 32.1 us
  Pallas kernels  24.7 us (76%)
  local copies, waits for them, and re-layouts  4.02 us (12%)
  other arithmetic  2.71 us (8%)
  between operations  0.68 us (2%)
    pallas_call x1, Pallas kernels, on_device(): pl.pallas_call(functools.partial(body, pn), out_shape=(jax.ShapeDtypeStru...  24.7 us
    another operation x3, other arithmetic, on_device(): jnp.stack([code.astype(F32), owner.astype(F32), alive, offset], axis=1)  2.04 us
    unnamed x8, local copies, waits for them, and re-layouts  1.42 us
    slice x1, local copies, waits for them, and re-layouts, on_device(): hamiltonian = packed[:, :pn.square].reshape(pn.pairs, pn.funcs, pn.funcs)  0.81 us
    concatenate x1, local copies, waits for them, and re-layouts, on_device(): jnp.concatenate([(kernel * alive[:, None, None]).reshape(pn.pairs, pn.squ...  0.7 us
    convert_element_type x1, other arithmetic, on_device(): (anchor - domain * pn.slab).astype(F32)  0.66 us

profile of v1, /device:TPU:0, one launch (start us, length us, event | category | flops | bytes accessed | tf_op | source)
XLA Modules:
  0.0 32.1 jit_solution(2618223185633713514)
XLA Ops:
  0.6 0.0 copy-start.1
  0.6 0.0 copy-start
  0.7 0.7 %convert_bitcast_fusion.1 = f32[32,1]{0,1:T(1,128)S(1)} fusion(s32[32]{0:T(128)} %param.11, s32[]{:T(128)S(6)} %axis_index.25), kind=kLoop, calls=%fused_computation.15 | loop fusion | flops 1120 | bytes 260 | tf_op jit(solution)/shard_map/stack | solution.py:341
  1.4 0.7 %convert_bitcast_fusion = f32[32,1]{0,1:T(1,128)S(1)} fusion(s32[32]{0:T(128)} %param.10, s32[]{:T(128)S(6)} %mul.25), kind=kLoop, calls=%fused_computation.14 | loop fusion | flops 64 | bytes 260 | tf_op jit(solution)/shard_map/stack | solution.py:341
  2.0 0.7 %subtract_convert_fusion = f32[8]{0:T(128)S(1)} fusion(s32[8]{0:T(128)} %param.8, s32[]{:T(128)S(6)} %mul.26), kind=kLoop, calls=%fused_computation.13 | loop fusion | flops 16 | bytes 68 | tf_op jit(solution)/shard_map/convert_element_type | solution.py:337
  2.7 0.7 %convert_bitcast_fusion.2 = (f32[32,1]{0,1:T(1,128)S(1)}, f32[32]{0:T(128)S(1)}) fusion(s32[32]{0:T(128)} %param.12), kind=kLoop, calls=%fused_computation.16 | loop fusion | flops 32 | bytes 384 | tf_op jit(solution)/shard_map/stack | solution.py:341
  3.4 0.1 copy.19
  3.5 0.1 copy.20
  3.5 0.1 copy.18
  3.6 0.1 copy.17
  3.7 0.0 copy-done.1
  3.7 0.1 copy.16
  3.8 0.7 %concatenate.3.meta_ref = f32[32,128]{1,0:T(8,128)} concatenate(f32[32,81]{1,0:T(8,128)S(1)} %copy.16, f32[32,1]{1,0:T(8,128)S(1)} %copy.17, f32[32,1]{1,0:T(8,128)S(1)} %copy.18, f32[32,1]{1,0:T(8,128)S(1)} %copy.19, f32[32,1]{1,0:T(8,128)S(1)} %copy.20, f32[32,43]{1,0:T(8,128)S(1)} %broadcast_in_dim.4), dimensions={1} | concatenate | bytes 32768 | tf_op jit(solution)/shard_map/concatenate | solution.py:338
  4.5 0.0 copy-done
  4.5 0.8 %copy.21.support_ref = bf16[8,9,15,128]{3,2,1,0:T(8,128)(2,1)} copy(bf16[8,9,15,128]{3,0,2,1:T(8,128)(2,1)S(1)} %copy-done) | data formatting | bytes 552960 | tf_op args[0]
  5.3 24.7 %grain.1 = (f32[16,128]{1,0:T(8,128)}, f32[32,128]{1,0:T(8,128)}) custom-call(f32[32,128]{1,0:T(8,128)} %concatenate.3.meta_ref, bf16[8,9,15,128]{3,2,1,0:T(8,128)(2,1)} %copy.21.support_ref, f32[16,128]{1,0:T(8,128)} %v_ref.1), custom_call_target="tpu_custom_call" | custom-call | tf_op jit(solution)/shard_map/grain/pallas_call | solution.py:350
  30.0 0.8 %copy.22 = f32[32,81]{0,1:T(8,128)S(1)} copy(f32[32,81]{1,0:T(8,128)} %bitcast.13) | data formatting | bytes 20736 | tf_op jit(solution)/shard_map/slice | solution.py:385
  30.8 0.0 copy-start.2
  30.8 0.6 %reshape.12 = f32[32,9,9]{0,2,1:T(8,128)} reshape(f32[32,81]{0,1:T(8,128)S(1)} %copy.22) | data formatting | bytes 20736 | tf_op jit(solution)/shard_map/reshape | solution.py:385
  31.5 0.1 copy-done.2
  31.5 0.6 %copy.24 = f32[16,128]{1,0:T(8,128)} copy(f32[16,128]{1,0:T(8,128)S(1)} %copy-done.2) | data formatting | bytes 16384
  (4 shorter events, 0.0 us)
Async XLA Ops:
  0.6 3.1 %copy-start.1 = (f32[32,9,9]{0,2,1:T(8,128)S(1)}, f32[32,9,9]{0,2,1:T(8,128)}, u32[]{:S(2)}) copy-start(f32[32,9,9]{0,2,1:T(8,128)} %param.9) | copy-start | bytes 31108
  0.6 3.9 %copy-start = (bf16[8,9,15,128]{3,0,2,1:T(8,128)(2,1)S(1)}, bf16[8,9,15,128]{3,0,2,1:T(8,128)(2,1)}, u32[]{:S(2)}) copy-start(bf16[8,9,15,128]{3,0,2,1:T(8,128)(2,1)} %param.7) | copy-start | bytes 829444
  30.8 0.7 %copy-start.2 = (f32[16,128]{1,0:T(8,128)S(1)}, f32[16,128]{1,0:T(8,128)}, u32[]{:S(2)}) copy-start(f32[16,128]{1,0:T(8,128)} %get-tuple-element.12) | copy-start | bytes 24580

commit v2 on v1

--- a/solution.py
+++ b/solution.py
@@ -19,11 +19,6 @@
 
 def dot_t(a, b):
     return lax.dot_general(a, b, (((1,), (1,)), ((), ())), preferred_element_type=F32)
-
-
-def split(value):
-    high = value.astype(BF16)
-    return high, (value - high.astype(F32)).astype(BF16)
 
 
 def respond(field):
@@ -61,12 +56,18 @@
 
 def body(
     pn,
-    meta_ref,
+    kernel_ref,
+    owner_ref,
+    partner_ref,
+    live_ref,
+    anchor_ref,
     support_ref,
     v_ref,
     density_ref,
     ham_ref,
-    pad,
+    turned,
+    meta_ref,
+    chooser,
     packed,
     boxes,
     metas,
@@ -112,14 +113,29 @@
                 )
                 met += 1
 
-    pad[...] = jnp.zeros_like(pad)
-    pad[:, :, 0 : pn.depth, :] = support_ref[...]
-    step = pad.shape[2]
-    lane = lax.broadcasted_iota(jnp.int32, (A, A * step), 1)
-    sub = lax.broadcasted_iota(jnp.int32, (A, A * step), 0)
-    j = lane - sub * step
-    mine = (j >= 0) & (j < pn.depth)
-    offset = jnp.broadcast_to(meta_ref[0:A, pn.square + 3 : pn.square + 4], (A, A * step))
+    domain_atoms = A * n
+    alive = live_ref[...].astype(F32)
+    turned[...] = jnp.zeros_like(turned)
+    for s in range(F):
+        turned[s * F : (s + 1) * F, 0 : pn.pairs] = kernel_ref[s] * alive
+    away = partner_ref[...] // domain_atoms
+    within = partner_ref[...] - away * domain_atoms
+    away = away - dom + 1
+    away = jnp.where(away < 0, away + space_count, away)
+    away = jnp.where(away >= space_count, away - space_count, away)
+    base = pn.square
+    turned[base : base + 1, 0 : pn.pairs] = (away * domain_atoms + within).astype(F32)
+    turned[base + 1 : base + 2, 0 : pn.pairs] = (owner_ref[...] - (dom * n + orb) * A).astype(F32)
+    turned[base + 2 : base + 3, 0 : pn.pairs] = alive
+    turned[base + 3 : base + 4, 0:A] = (anchor_ref[...] - dom * pn.slab).astype(F32)
+    meta_ref[...] = turned[...].T[0 : pn.pairs]
+
+    held = pn.depth * A
+    lane = lax.broadcasted_iota(jnp.int32, (A, held), 1)
+    sub = lax.broadcasted_iota(jnp.int32, (A, held), 0)
+    j = lane // A
+    mine = lane - j * A == sub
+    offset = jnp.broadcast_to(meta_ref[0:A, pn.square + 3 : pn.square + 4], (A, held))
     spot = offset.astype(jnp.int32) + j
     place_rows = []
     for o in range(n):
@@ -130,7 +146,8 @@
     placing = jnp.concatenate(place_rows, axis=0).astype(BF16)
     aligned = []
     for s in range(F):
-        aligned.append(dot(placing, pad[:, s].reshape(A * step, Q)))
+        rows = support_ref[s].astype(F32).reshape(held, Q).astype(BF16)
+        aligned.append(dot(placing, rows))
     nothing = jnp.zeros((A, Q), F32)
     for o in range(n):
         for i in range(pn.rows):
@@ -179,6 +196,24 @@
                 packed.at[orb, :, cols], boxes.at[orb, :, cols],
                 zs_sem.at[0, c], zr_sem.at[orb, c], {"space": above},
             )
+    everyone = pn.blocks * pn.pairs
+
+    def columns(shape, axis):
+        col = lax.broadcasted_iota(jnp.int32, shape, axis)
+        blk = jnp.zeros(shape, jnp.int32)
+        for b in range(1, pn.blocks):
+            blk = blk + jnp.where(col >= b * pn.block, 1, 0)
+        rest = col - blk * pn.block
+        func = rest // A
+        return blk * A + (rest - func * A), func
+
+    code, func = columns((1, pn.total), 1)
+    gather_col = lax.broadcasted_iota(jnp.int32, (pn.total, LANES), 1)
+    _, gather_func = columns((pn.total, 1), 0)
+    gather_func = jnp.where(gather_func < F, gather_func, -pn.square)
+    gather_diff = gather_col - gather_func
+    for s in range(F):
+        chooser[s] = jnp.where(gather_diff == s * F, 1.0, 0.0).astype(BF16)
     boxes[n + orb] = packed[orb]
     metas[n + orb] = meta_ref[...]
     for c, (lo, hi) in enumerate(pn.chunks):
@@ -197,57 +232,37 @@
     for o in range(n):
         arrive(metas.at[o], ms_sem.at[n], mr_sem.at[o])
 
-    everyone = pn.blocks * pn.pairs
     table = metas[...].reshape(everyone, LANES)
     holder = lax.broadcasted_iota(jnp.int32, (everyone, 1), 0) // pn.pairs
     partner = table[:, pn.square : pn.square + 1].astype(jnp.int32)
     partner = partner - jnp.where(holder < n, n * A, 0)
     owner = table[:, pn.square + 1 : pn.square + 2].astype(jnp.int32) + holder * A
-
-    def columns(shape, axis):
-        col = lax.broadcasted_iota(jnp.int32, shape, axis)
-        blk = jnp.zeros(shape, jnp.int32)
-        for b in range(1, pn.blocks):
-            blk = blk + jnp.where(col >= b * pn.block, 1, 0)
-        rest = col - blk * pn.block
-        func = rest // A
-        return blk * A + (rest - func * A), func
-
-    code, func = columns((everyone, pn.total), 1)
     picks = jnp.where((code == partner) & (func < F), 1.0, 0.0)
     picks16 = picks.astype(BF16)
     owner_lane = lax.broadcasted_iota(jnp.int32, (everyone, LANES), 1)
     owns = jnp.where(owner_lane == owner, 1.0, 0.0)
     owns_t = owns.T[0 : pn.blocks * A].astype(BF16)
     owns16 = owns[:, 0 : pn.blocks * A].astype(BF16)
-    table_hi, table_lo = split(table)
+    table16 = table.astype(BF16)
     spread_row = lax.broadcasted_iota(jnp.int32, (LANES, pn.total), 0)
-    _, spread_func = columns((LANES, pn.total), 1)
-    spread_func = jnp.where(spread_func < F, spread_func, -pn.square)
-    kmat[...] = jnp.zeros_like(kmat)
+    spread_diff = spread_row - jnp.where(func < F, func, -pn.square)
+    for b in range(pn.blocks):
+        kmat[b * pn.block + F * A : (b + 1) * pn.block, :] = jnp.zeros(
+            (pn.block - F * A, pn.total), F32
+        )
     for s in range(F):
-        spread = jnp.where(spread_row == s * F + spread_func, 1.0, 0.0).astype(BF16)
-        q_hi = dot(table_hi, spread).astype(BF16) * picks16
-        q_lo = dot(table_lo, spread).astype(BF16) * picks16
-        rows = dot(owns_t, q_hi) + dot(owns_t, q_lo)
+        spread = jnp.where(spread_diff == s * F, 1.0, 0.0).astype(BF16)
+        rows = dot(owns_t, dot(table16, spread).astype(BF16) * picks16)
         for b in range(pn.blocks):
             kmat[b * pn.block + s * A : b * pn.block + (s + 1) * A, :] = rows[b * A : (b + 1) * A]
-    k_hi, k_lo = split(kmat[...])
-
-    for k in range(n):
-        other = peer(k)
-        for c, (lo, hi) in enumerate(pn.chunks[:2]):
-            cols = pl.ds(lo * Q, (hi - lo) * Q)
-            arrive(boxes.at[other, :, cols], zs_sem.at[k, c], zr_sem.at[other, c])
-
-    for b in range(pn.blocks):
+    k16 = kmat[...].astype(BF16)
+    low = n * pn.block
+
+    def keep_planes(b, lo, hi):
         start = jnp.broadcast_to(metas[b, 0:A, pn.square + 3 : pn.square + 4], (A, Q))
         start = jnp.concatenate([start] * 2, axis=0).astype(jnp.int32)
-        for i in range(pn.rows):
+        for i in range(lo, hi):
             cols = slice(i * Q, (i + 1) * Q)
-            if b < n and i >= pn.zrows:
-                masked[b * pn.block : (b + 1) * pn.block, cols] = jnp.zeros((pn.block, Q), BF16)
-                continue
             r = pn.plane(orb, i)
             keep = (start <= r) if b >= n else (start > r)
             for t in range(pn.block // (2 * A)):
@@ -256,32 +271,42 @@
                     keep, part, 0.0
                 ).astype(BF16)
 
-    aux[...] = dot(k_hi, masked[...]) + dot(k_lo, masked[...])
-    for i in range(pn.rows):
-        cols = slice(i * Q, (i + 1) * Q)
-        x = masked[:, cols].astype(F32)
-        line = jnp.sum(x * aux[:, cols], axis=0, keepdims=True)
-        dens[orb, pl.ds(i, 1), :] = line
-        potential = v_ref[pl.ds(pn.plane(orb, i), 1), :] + respond(line)
-        weighted[:, cols] = (x * potential).astype(BF16)
+    for b in range(n, pn.blocks):
+        keep_planes(b, 0, pn.rows)
+    aux[...] = dot(k16[:, low:], masked[low:, :])
+    gmat[...] = jnp.zeros_like(gmat)
+    for c in list(range(2, len(pn.chunks))) + [0, 1]:
+        lo, hi = pn.chunks[c]
+        span = slice(lo * Q, hi * Q)
+        if c < 2:
+            cols = pl.ds(lo * Q, (hi - lo) * Q)
+            for k in range(n):
+                other = peer(k)
+                arrive(boxes.at[other, :, cols], zs_sem.at[k, c], zr_sem.at[other, c])
+            for b in range(n):
+                keep_planes(b, lo, hi)
+            aux[:, span] = aux[:, span] + dot(k16[:, :low], masked[:low, span])
+        else:
+            masked[:low, span] = jnp.zeros((low, (hi - lo) * Q), BF16)
+        for i in range(lo, hi):
+            cols = slice(i * Q, (i + 1) * Q)
+            x = masked[:, cols].astype(F32)
+            line = jnp.sum(x * aux[:, cols], axis=0, keepdims=True)
+            dens[orb, pl.ds(i, 1), :] = line
+            potential = v_ref[pl.ds(pn.plane(orb, i), 1), :] + respond(line)
+            weighted[:, cols] = (x * potential).astype(BF16)
+        gmat[...] = gmat[...] + dot_t(weighted[:, span], masked[:, span])
     for k in range(1, n):
         send(dens.at[orb], dens.at[orb], ds_sem.at[k], dr_sem.at[orb], {"orb": peer(k)})
-    gmat[...] = dot_t(weighted[...], masked[...])
-
-    gather_col = lax.broadcasted_iota(jnp.int32, (pn.total, LANES), 1)
-    _, gather_func = columns((pn.total, LANES), 0)
-    gather_func = jnp.where(gather_func < F, gather_func, -pn.square)
+
     found = jnp.zeros((everyone, LANES), F32)
     for s in range(F):
         rows = jnp.concatenate(
             [gmat[b * pn.block + s * A : b * pn.block + (s + 1) * A, :] for b in range(pn.blocks)],
             axis=0,
-        )
-        r_hi, r_lo = split(rows)
-        t_hi, t_lo = split((dot(owns16, r_hi) + dot(owns16, r_lo)) * picks)
-        gather = jnp.where(gather_col == s * F + gather_func, 1.0, 0.0).astype(BF16)
-        found = found + dot(t_hi, gather) + dot(t_lo, gather)
-    hpart[...] = found.reshape(pn.blocks, pn.pairs, LANES)
+        ).astype(BF16)
+        found = found + dot(dot(owns16, rows).astype(BF16) * picks16, chooser[s])
+    hpart[...] = found.astype(BF16).reshape(pn.blocks, pn.pairs, LANES)
 
     count = 0
     for up in (1, 0):
@@ -315,48 +340,39 @@
                     continue
                 slot = (up * n + peer(k)) * 2 + lax.rem(grid + g, 2)
                 arrive(hrecv.at[slot], hs_sem.at[0], hr_sem.at[slot])
-    total = hrecv[0]
+    total = hrecv[0].astype(F32)
     for slot in range(1, 2 * pn.blocks):
-        total = total + hrecv[slot]
+        total = total + hrecv[slot].astype(F32)
     ham_ref[...] = total * meta_ref[:, pn.square + 2 : pn.square + 3]
     for copy in sends:
         copy.wait_send()
 
 
+def finish(pn, plane_ref, block_ref, density_ref, ham_ref):
+    density_ref[...] = plane_ref[...]
+    rows = block_ref[...].T
+    for s in range(pn.funcs):
+        ham_ref[s] = rows[s * pn.funcs : (s + 1) * pn.funcs, :]
+
+
 def on_device(support, anchor, kernel, pair_owner, pair_partner, pair_live, v_ext):
     orb_count, space_count = lax.axis_size("orb"), lax.axis_size("space")
     pn = Plan(support, kernel, v_ext, orb_count, space_count)
-    domain, orb_index = lax.axis_index("space"), lax.axis_index("orb")
-    per_domain = pn.atoms * orb_count
-    own_block = domain * orb_count + orb_index
-    partner_domain = pair_partner // per_domain
-    relative = (partner_domain - domain + 1 + space_count) % space_count
-    code = relative * per_domain + pair_partner % per_domain
-    owner = pair_owner - own_block * pn.atoms
-    alive = pair_live.astype(F32)
-    offset = jnp.pad((anchor - domain * pn.slab).astype(F32), (0, pn.pairs - pn.atoms))
-    meta = jnp.concatenate(
-        [
-            (kernel * alive[:, None, None]).reshape(pn.pairs, pn.square),
-            jnp.stack([code.astype(F32), owner.astype(F32), alive, offset], axis=1),
-            jnp.zeros((pn.pairs, LANES - pn.square - 4), F32),
-        ],
-        axis=1,
-    )
     n, C = pn.orbs, len(pn.chunks)
     vmem = pl.BlockSpec(memory_space=pltpu.VMEM)
     dma = pltpu.SemaphoreType.DMA
-    step = -(-pn.depth // 16) * 16
     density, packed = pl.pallas_call(
         functools.partial(body, pn),
         out_shape=(
             jax.ShapeDtypeStruct(v_ext.shape, F32),
             jax.ShapeDtypeStruct((pn.pairs, LANES), F32),
         ),
-        in_specs=[vmem] * 3,
+        in_specs=[vmem] * 7,
         out_specs=(vmem, vmem),
         scratch_shapes=[
-            pltpu.VMEM((pn.atoms, pn.funcs, step, pn.points), BF16),
+            pltpu.VMEM((LANES, LANES), F32),
+            pltpu.VMEM((pn.pairs, LANES), F32),
+            pltpu.VMEM((pn.funcs, pn.total, LANES), BF16),
             pltpu.VMEM((n, pn.block, pn.width), BF16),
             pltpu.VMEM((pn.blocks, pn.block, pn.width), BF16),
             pltpu.VMEM((pn.blocks, pn.pairs, LANES), F32),
@@ -366,8 +382,8 @@
             pltpu.VMEM((pn.total, pn.total), F32),
             pltpu.VMEM((pn.total, pn.width), BF16),
             pltpu.VMEM((n, pn.rows, pn.points), F32),
-            pltpu.VMEM((pn.blocks, pn.pairs, LANES), F32),
-            pltpu.VMEM((2 * pn.blocks, pn.pairs, LANES), F32),
+            pltpu.VMEM((pn.blocks, pn.pairs, LANES), BF16),
+            pltpu.VMEM((2 * pn.blocks, pn.pairs, LANES), BF16),
             dma((n, C)),
             dma((n, C)),
             dma((n, 2)),
@@ -381,9 +397,26 @@
         ],
         compiler_params=pltpu.CompilerParams(collective_id=0, has_side_effects=True),
         name="grain",
-    )(meta, support, v_ext)
-    hamiltonian = packed[:, : pn.square].reshape(pn.pairs, pn.funcs, pn.funcs)
-    return (density, hamiltonian)
+    )(
+        jnp.transpose(kernel, (1, 2, 0)),
+        pair_owner.reshape(1, pn.pairs),
+        pair_partner.reshape(1, pn.pairs),
+        pair_live.reshape(1, pn.pairs),
+        anchor.reshape(1, pn.atoms),
+        jnp.transpose(support, (1, 2, 0, 3)),
+        v_ext,
+    )
+    density, blocks = pl.pallas_call(
+        functools.partial(finish, pn),
+        out_shape=(
+            jax.ShapeDtypeStruct(v_ext.shape, F32),
+            jax.ShapeDtypeStruct((pn.funcs, pn.funcs, pn.pairs), F32),
+        ),
+        in_specs=[vmem] * 2,
+        out_specs=(vmem, vmem),
+        name="finish",
+    )(density, packed)
+    return (density, jnp.transpose(blocks, (2, 0, 1)))
 
 
 def solution(mesh):

time: 32.5 us -> 24.9 us (0.77)
  local copies, waits for them, and re-layouts: 4.02 us -> 0 us
  other arithmetic: 2.71 us -> 0 us
  Pallas kernels: 24.7 us -> 24 us
    pallas_call x1, Pallas kernels: 24.7 us -> 22.5 us  [on_device(): pl.pallas_call(functools.partial(body, pn), out_shape=(jax.ShapeDtypeStru...]
    another operation x3 -> x0, other arithmetic: 2.04 us -> none  [on_device(): jnp.stack([code.astype(F32), owner.astype(F32), alive, offset], axis=1)]
    pallas_call x0 -> x1, Pallas kernels: none -> 1.46 us  [on_device(): pl.pallas_call(functools.partial(finish, pn), out_shape=(jax.ShapeDtypeSt...]
    unnamed x8 -> x0, local copies, waits for them, and re-layouts: 1.42 us -> none
    slice x1 -> x0, local copies, waits for them, and re-layouts: 0.81 us -> none  [on_device(): hamiltonian = packed[:, :pn.square].reshape(pn.pairs, pn.funcs, pn.funcs)]
    reshape x3 -> x0, local copies, waits for them, and re-layouts: 0.72 us -> none  [the longest x1 0.64 us: on_device(): hamiltonian = packed[:, :pn.square].reshape(pn.pairs, pn.funcs, pn.funcs)]
    concatenate x1 -> x0, local copies, waits for them, and re-layouts: 0.7 us -> none  [on_device(): jnp.concatenate([(kernel * alive[:, None, None]).reshape(pn.pairs, pn.squ...]
    convert_element_type x1 -> x0, other arithmetic: 0.66 us -> none  [on_device(): (anchor - domain * pn.slab).astype(F32)]
where the time goes in v2:
time: 24.9 us; the launch traced here: 24.6 us
  Pallas kernels  24 us (96%)
  between operations  0.64 us (3%)
    pallas_call x1, Pallas kernels, on_device(): pl.pallas_call(functools.partial(body, pn), out_shape=(jax.ShapeDtypeStru...  22.5 us
    pallas_call x1, Pallas kernels, on_device(): pl.pallas_call(functools.partial(finish, pn), out_shape=(jax.ShapeDtypeSt...  1.46 us

profile of v2, /device:TPU:0, one launch (start us, length us, event | category | flops | bytes accessed | tf_op | source)
XLA Modules:
  0.0 24.6 jit_solution(12318133484062527407)
XLA Ops:
  0.6 22.5 %grain.1 = (f32[16,128]{1,0:T(8,128)}, f32[32,128]{1,0:T(8,128)}) custom-call(f32[9,9,32]{2,1,0:T(8,128)} %bitcast.8, s32[1,32]{1,0:T(1,128)} %bitcast.9, s32[1,32]{1,0:T(1,128)} %bitcast.10, s32[1,32]{1,0:T(1,128)} %bitcast.11, s32[1,8]{1,0:T(1,128)} %bitcast.12, bf16[9,15,8,128]{3,2,1,0:T(8,128)(2,1)} %bitcast.7, f32[16,128]{1,0:T(8,128)} %v_ref.1), custom_call_target="tpu_custom_call" | custom-call | tf_op jit(solution)/shard_map/grain/pallas_call | solution.py:364
  23.2 1.5 %finish.1 = (f32[16,128]{1,0:T(8,128)}, f32[9,9,32]{2,1,0:T(8,128)}) custom-call(f32[16,128]{1,0:T(8,128)} %get-tuple-element.6.plane_ref, f32[32,128]{1,0:T(8,128)} %get-tuple-element.7.block_ref), custom_call_target="tpu_custom_call" | custom-call | tf_op jit(solution)/shard_map/finish/pallas_call | solution.py:409
